TPU v7x, 32 devices: a whole 2x2x4 slice. The times are simulated.
32 devices in a mesh: groups: 2 (over x), seq: 4 (over z), expert: 4 (over y, core).
Axes of the slice: x: 2, y: 2, z: 4, core: 2. Of those that a mesh axis runs over, the one named last changes fastest.
Arguments:
- q_lat: bfloat16 [512, 65536], P(('groups', 'seq'), 'expert'), parts along dimension 0, may hold values from -36 to 36
- q_rope: bfloat16 [512, 8192], P(('groups', 'seq'), 'expert'), parts along dimension 0, may hold values from -6 to 6
- cache_lat: bfloat16 [2048, 512], P(('groups', 'seq')), parts along dimension 0, may hold values from -7 to 7
- cache_rope: bfloat16 [2048, 64], P(('groups', 'seq')), parts along dimension 0, may hold values from -8 to 8
- tool_lat: bfloat16 [256, 512], P(('groups', 'seq')), parts along dimension 0, may hold values from -2.5 to 2.5
- tool_rope: bfloat16 [256, 64], P(('groups', 'seq')), parts along dimension 0, may hold values from -8 to 8
- offset: int32 [2], P('groups'), parts along dimension 0, may hold values from 512 to 736
- suf_lat: bfloat16 [512, 512], P(('groups', 'seq')), parts along dimension 0, may hold values from -6 to 6
- suf_rope: bfloat16 [512, 64], P(('groups', 'seq')), parts along dimension 0, may hold values from -8 to 8
- w_uv: bfloat16 [128, 512, 128], P('expert'), may hold values from -1 to 1
- w_out: bfloat16 [16384, 7168], P('expert', 'seq'), may hold values from -0.19921875 to 0.19921875
- resid: bfloat16 [512, 7168], P(('groups', 'expert'), 'seq'), parts along dimension 0, may hold values from -36 to 36
- routes: int32 [512, 2], P(('groups', 'expert')), parts along dimension 0, may hold values from 0 to 3, all different within a row; in each aligned block of 64 rows (0 to 63, 64 to 127, ...) at most 40 rows name the same one
- probs: float32 [512, 2], P(('groups', 'expert')), parts along dimension 0, may hold values from 0.1 to 1
- w_gate: bfloat16 [4, 7168, 1024], P('expert', None, 'seq'), may hold values from -0.0625 to 0.0625
- w_up: bfloat16 [4, 7168, 1024], P('expert', None, 'seq'), may hold values from -0.0625 to 0.0625
- w_down: bfloat16 [4, 1024, 7168], P('expert', 'seq'), may hold values from -0.1875 to 0.1875
Outputs:
- attn_residual: bfloat16 [512, 7168], P(('groups', 'expert'), 'seq'), parts along dimension 0
- expert_mix: bfloat16 [512, 7168], P(('groups', 'expert'), 'seq'), parts along dimension 0
There are 2 independent parts, one for each index of `groups`. A program takes and returns all parts, laid end to end along the dimension named above; an argument that names none is the same for every part. Nothing has to cross between parts.
Inputs may be any that keep to these rules, and one draw needn't show every extreme that they name: `routes`: within the rows of one device of the expert axis (64 rows in a row), no expert is named more than 40 times.
All inputs are finite; a program needn't handle non-finite values.
Results may differ from a plain program's by a relative error of at most 0.03.
Values may be sent and summed in bfloat16 or wider, within the bound.
No kernel may reach another device: no remote copies, remote signals or barrier semaphores. Data moves between devices by JAX's collectives and lax.ppermute only.
A program may use at most 128 MiB of HBM per device.

v0:
```python
import jax
import jax.numpy as jnp
from jax import lax
from jax.sharding import PartitionSpec as P

score_scale = 192.0 ** (-0.5)
floor_score = -1e30
norm_eps = 1e-06


def run_expert(tokens_in, w_gate, w_up, w_down):
    sources, count, width = tokens_in.shape
    rows = tokens_in.reshape(sources * count, width)
    gate = jnp.dot(rows, w_gate[0], preferred_element_type=jnp.float32)
    upper = jnp.dot(rows, w_up[0], preferred_element_type=jnp.float32)
    inner = (jax.nn.silu(gate) * upper).astype(jnp.bfloat16)
    partial_out = jnp.dot(inner, w_down[0], preferred_element_type=jnp.float32).reshape(
        sources, count, width
    )
    summed = lax.psum_scatter(
        partial_out.astype(jnp.bfloat16), "seq", scatter_dimension=2, tiled=True
    )
    return lax.all_to_all(summed, "expert", split_axis=0, concat_axis=0, tiled=True)


def on_device(
    q_lat,
    q_rope,
    cache_lat,
    cache_rope,
    tool_lat,
    tool_rope,
    offset,
    suf_lat,
    suf_rope,
    w_uv,
    w_out,
    resid,
    routes,
    probs,
    w_gate,
    w_up,
    w_down,
):
    seq_index = lax.axis_index("seq")
    ctx_dev = cache_lat.shape[0]
    query_dev = q_lat.shape[0]
    heads_dev, lat_width, value_width = w_uv.shape
    rope_width = cache_rope.shape[1]
    tool_all_lat, tool_all_rope = (
        lax.all_gather(tool_lat, "seq", axis=0, tiled=True),
        lax.all_gather(tool_rope, "seq", axis=0, tiled=True),
    )
    tool_len = tool_all_lat.shape[0]
    position = seq_index * ctx_dev + jnp.arange(ctx_dev, dtype=jnp.int32)
    shifted = position - offset[0]
    inside = (shifted >= 0) & (shifted < tool_len)
    safe = jnp.clip(shifted, 0, tool_len - 1)
    ctx_lat = jnp.where(inside[:, None], jnp.take(tool_all_lat, safe, axis=0), cache_lat)
    ctx_rope = jnp.where(inside[:, None], jnp.take(tool_all_rope, safe, axis=0), cache_rope)
    local_lat = jnp.concatenate([ctx_lat, suf_lat], axis=0)
    local_rope = jnp.concatenate([ctx_rope, suf_rope], axis=0)
    block_len = ctx_dev + query_dev
    query_rows = query_dev * heads_dev
    queries_lat = q_lat.reshape(query_rows, lat_width)
    queries_rope = q_rope.reshape(query_rows, rope_width)
    query_pos = seq_index * query_dev + jnp.arange(query_rows, dtype=jnp.int32) // heads_dev
    running_max = jnp.full((query_rows,), floor_score, jnp.float32)
    piece_lat = lax.all_gather(local_lat, "seq", axis=0, tiled=True)
    piece_rope = lax.all_gather(local_rope, "seq", axis=0, tiled=True)
    global_row = jnp.arange(piece_lat.shape[0], dtype=jnp.int32)
    within = global_row % block_len
    owner = global_row // block_len
    is_context = within < ctx_dev
    suffix_pos = owner * query_dev + within - ctx_dev
    visible = is_context[None, :] | (suffix_pos[None, :] <= query_pos[:, None])
    scores = jnp.einsum("qc,kc->qk", queries_lat, piece_lat, preferred_element_type=jnp.float32)
    scores = (
        scores
        + jnp.einsum("qc,kc->qk", queries_rope, piece_rope, preferred_element_type=jnp.float32)
    ) * score_scale
    scores = jnp.where(visible, scores, floor_score)
    new_max = jnp.maximum(running_max, jnp.max(scores, axis=1))
    weights = jnp.where(visible, jnp.exp(scores - new_max[:, None]), 0.0)
    new_total = jnp.sum(weights, axis=1)
    new_acc = jnp.dot(weights.astype(jnp.bfloat16), piece_lat, preferred_element_type=jnp.float32)
    latent_out = (
        (new_acc / new_total[:, None]).astype(jnp.bfloat16).reshape(query_dev, heads_dev, lat_width)
    )
    head_vals = jnp.einsum(
        "thc,hcv->thv", latent_out, w_uv, preferred_element_type=jnp.float32
    ).astype(jnp.bfloat16)
    head_vals = head_vals.reshape(query_dev, heads_dev * value_width)
    all_values = lax.all_gather(head_vals, "seq", axis=0, tiled=True)
    tok_dev = resid.shape[0]
    attn_sum = lax.psum_scatter(
        jnp.dot(all_values, w_out, preferred_element_type=jnp.float32).astype(jnp.bfloat16),
        "expert",
        scatter_dimension=0,
        tiled=True,
    ).astype(jnp.float32)
    attn_residual = (resid.astype(jnp.float32) + attn_sum).astype(jnp.bfloat16)
    expert_count = lax.axis_size("expert") * w_gate.shape[0]
    top_count = routes.shape[1]
    capacity = tok_dev * top_count * 5 // (4 * expert_count)
    flat_routes = routes.reshape(-1)
    one_hot = (flat_routes[:, None] == jnp.arange(expert_count, dtype=jnp.int32)[None, :]).astype(
        jnp.int32
    )
    earlier = jnp.cumsum(one_hot, axis=0) - one_hot
    slot = jnp.sum(earlier * one_hot, axis=1)
    target = (flat_routes * capacity + slot).reshape(tok_dev, top_count)
    slot_ids = jnp.arange(expert_count * capacity, dtype=jnp.int32)
    matches = slot_ids[:, None, None] == target[None, :, :]
    send_matrix = jnp.any(matches, axis=2).astype(jnp.bfloat16)
    route_weight = 2.5 * probs / jnp.sum(probs, axis=1, keepdims=True)
    gather_matrix = jnp.sum(jnp.where(matches, route_weight[None, :, :], 0.0), axis=2).T
    whole_stream = lax.all_gather(attn_residual, "seq", axis=1, tiled=True).astype(jnp.float32)
    normed = (
        whole_stream
        * lax.rsqrt(jnp.mean(whole_stream * whole_stream, axis=1, keepdims=True) + norm_eps)
    ).astype(jnp.bfloat16)
    outgoing = jnp.dot(send_matrix, normed, preferred_element_type=jnp.float32).astype(jnp.bfloat16)
    outgoing = outgoing.reshape(expert_count, capacity, normed.shape[1])
    returned = run_expert(
        lax.all_to_all(outgoing, "expert", split_axis=0, concat_axis=0, tiled=True),
        w_gate,
        w_up,
        w_down,
    )
    returned = returned.reshape(expert_count * capacity, returned.shape[2]).astype(jnp.float32)
    expert_mix = jnp.dot(
        gather_matrix, returned, precision=lax.Precision.HIGHEST, preferred_element_type=jnp.float32
    )
    return (attn_residual, expert_mix.astype(jnp.bfloat16))


def solution(mesh):
    placed = (
        P(("groups", "seq"), "expert"),
        P(("groups", "seq"), "expert"),
        P(("groups", "seq"), None),
        P(("groups", "seq"), None),
        P(("groups", "seq"), None),
        P(("groups", "seq"), None),
        P("groups"),
        P(("groups", "seq"), None),
        P(("groups", "seq"), None),
        P("expert", None, None),
        P("expert", "seq"),
        P(("groups", "expert"), "seq"),
        P(("groups", "expert"), None),
        P(("groups", "expert"), None),
        P("expert", None, "seq"),
        P("expert", None, "seq"),
        P("expert", "seq", None),
    )
    return jax.shard_map(
        on_device,
        mesh=mesh,
        in_specs=placed,
        out_specs=(P(("groups", "expert"), "seq"), P(("groups", "expert"), "seq")),
        check_vma=False,
    )
```

profile of v0, /device:TPU:0, one launch (start us, length us, event | category | flops | bytes accessed | tf_op | source)
XLA Modules:
  0.0 289.8 jit_solution(17597389861939251030)
XLA Ops:
  7.2 0.0 all-gather.4.cloned.1.call-start
  8.1 15.3 %all_gather.18 = bf16[128,512]{1,0:T(8,128)(2,1)S(1)} all-gather(bf16[32,512]{1,0:T(8,128)(2,1)} %param.21), channel_id=1, replica_groups=mesh['groups'=2,'seq'=4,'expert'=4] {'seq'}, dimensions={0}, use_global_device_ids=true | all-gather | bytes 163840 | tf_op jit(solution)/shard_map/all_gather | solution.py:51
  23.4 1.2 gather_fusion
  24.5 0.0 copy-start.6
  24.5 0.0 copy-start.7
  24.5 1.1 select_select_fusion
  25.6 0.0 copy-start.4
  25.7 1.6 pad_maximum_fusion
  27.3 0.0 all-gather.4.cloned.1.call-update
  27.3 0.0 all-gather.6.cloned.1.call-start
  27.4 0.0 copy-done.2
  27.4 2.4 reshape.119
  29.7 13.2 %all_gather.20 = bf16[128,64]{1,0:T(8,128)(2,1)S(1)} all-gather(bf16[32,64]{1,0:T(8,128)(2,1)S(1)} %copy-done.8), channel_id=1, replica_groups=mesh['groups'=2,'seq'=4,'expert'=4] {'seq'}, dimensions={0}, use_global_device_ids=true | all-gather | bytes 20480 | tf_op jit(solution)/shard_map/all_gather | solution.py:52
  43.0 0.9 gather_fusion.1
  43.9 0.1 copy.58
  44.0 0.1 select_select_fusion.1
  44.2 0.1 copy.59
  44.3 15.6 %all-gather = bf16[4,320,64]{1,2,0:T(8,128)(2,1)S(1)} all-gather(bf16[1,320,64]{1,2,0:T(8,128)(2,1)S(1)} %copy.59), channel_id=1, replica_groups=mesh['groups'=2,'seq'=4,'expert'=4] {'seq'}, dimensions={0}, use_global_device_ids=true | all-gather | bytes 204800 | tf_op jit(solution)/shard_map/all_gather | solution.py:70
  59.8 0.2 copy.60
  60.0 0.2 reshape.143
  60.2 0.5 reshape.120
  60.8 3.9 %all-gather.4.cloned.1.call-done = bf16[1280,512]{1,0:T(8,128)(2,1)} async-done(((bf16[320,512]{1,0:T(8,128)(2,1)}), bf16[1280,512]{1,0:T(8,128)(2,1)}) %all-gather.4.cloned.1.call-update) | async-done | bytes 1310736 | tf_op jit(solution)/shard_map/all_gather | solution.py:69
  64.7 5.0 %fusion.51 = f32[1280,2048]{1,0:T(8,128)S(1)} fusion(bf16[1280,512]{1,0:T(8,128)(2,1)} %all-gather.4.cloned.1.call-done, bf16[2048,512]{1,0:T(8,128)(2,1)} %reshape.119), kind=kOutput, calls=%fused_computation.80 | convolution fusion | flops 2684354560 | bytes 13893632 | tf_op jit(solution)/shard_map/qc,kc->qk/dot_general | solution.py:77
  69.6 4.1 %fusion.50 = (f32[2048]{0:T(1024)S(1)}, f32[2048,1280]{0,1:T(8,128)S(1)}) fusion(f32[1280,2048]{1,0:T(8,128)S(1)} %fusion.51, bf16[1280,64]{0,1:T(8,128)(2,1)S(1)} %reshape.143, bf16[2048,64]{1,0:T(8,128)(2,1)S(1)} %reshape.120, s32[2048]{0:T(1024)S(1)} %fusion.40, s32[1280]{0:T(1024)S(1)} %fusion.38, pred[1280]{0:T(1024)(128)(4,1)S(1)} %fusion.45), kind=kOutput, calls=%fused_computation.79 | convolution fusion | flops 351270912 | bytes 21420288 | tf_op jit(solution)/shard_map/qc,kc->qk/dot_general | solution.py:80
  73.7 3.9 %fusion = f32[2048]{0:T(1024)S(1)} fusion(f32[2048,1280]{0,1:T(8,128)S(1)} %get-tuple-element.3, f32[2048]{0:T(1024)S(1)} %broadcast_maximum_fusion, s32[2048]{0:T(1024)S(1)} %fusion.40, s32[1280]{0:T(1024)S(1)} %fusion.38, pred[1280]{0:T(1024)(128)(4,1)S(1)} %fusion.45), kind=kLoop, calls=%fused_computation.7 | loop fusion | flops 13105152 | bytes 10516736 | tf_op jit(solution)/shard_map/reduce_sum | solution.py:85
  77.7 0.0 copy-start
  77.7 4.5 %divide_convert_fusion = bf16[2048,512]{1,0:T(8,128)(2,1)S(1)} fusion(f32[2048]{0:T(1024)S(1)} %fusion, bf16[1280,512]{1,0:T(8,128)(2,1)S(1)} %copy-done.13, f32[2048,1280]{0,1:T(8,128)S(1)} %get-tuple-element.3, f32[2048]{0:T(1024)S(1)} %broadcast_maximum_fusion, s32[2048]{0:T(1024)S(1)} %fusion.40, s32[1280]{0:T(1024)S(1)} %fusion.38, ...), kind=kOutput, calls=%fused_computation.15 | convolution fusion | flops 2699558912 | bytes 13924608 | tf_op jit(solution)/shard_map/dot_general | solution.py:86
  82.3 2.5 fusion.23
  84.8 0.9 copy.73
  85.7 0.0 all-gather.6.cloned.1.call-update
  85.7 0.0 copy-start.9
  85.7 0.0 copy-start.5
  85.7 0.0 reduce-scatter.3.cloned.1.call-start
  85.8 44.8 %all-gather.6.cloned.1.call-done = bf16[256,4096]{1,0:T(8,128)(2,1)} async-done(((bf16[64,4096]{1,0:T(8,128)(2,1)}), bf16[256,4096]{1,0:T(8,128)(2,1)}) %all-gather.6.cloned.1.call-update) | async-done | bytes 2097168 | tf_op jit(solution)/shard_map/all_gather | solution.py:94
  130.6 10.7 %convolution_convert_fusion.2 = bf16[256,1792]{1,0:T(8,128)(2,1)} fusion(bf16[256,4096]{1,0:T(8,128)(2,1)} %all-gather.6.cloned.1.call-done, bf16[4096,1792]{1,0:T(8,128)(2,1)} %param.27), kind=kOutput, calls=%fused_computation.21 | convolution fusion | flops 3758555136 | bytes 17694720 | tf_op jit(solution)/shard_map/dot_general | solution.py:97
  141.3 0.0 reduce-scatter.3.cloned.1.call-update
  141.4 0.3 reduce-scatter.5.cloned.1.call-start
  141.6 0.1 copy.63
  141.7 0.1 eq.31
  141.9 0.1 fusion.35
  142.0 0.2 reduce_window_sum.11
  142.1 0.2 select_reduce_fusion.1
  142.3 0.1 reduce_sum.49
  142.5 0.1 copy.64
  142.6 0.1 fusion.34
  142.7 21.6 %reduce-scatter.3.cloned.1.call-done = bf16[64,1792]{1,0:T(8,128)(2,1)} async-done(((bf16[256,1792]{1,0:T(8,128)(2,1)}), bf16[64,1792]{1,0:T(8,128)(2,1)}) %reduce-scatter.3.cloned.1.call-update) | async-done | bytes 229392 | tf_op jit(solution)/shard_map/reduce_scatter | solution.py:96
  164.3 1.0 add_convert_fusion
  165.3 0.0 copy-start.3
  165.3 21.0 %all_gather.23 = bf16[64,7168]{1,0:T(8,128)(2,1)S(1)} all-gather(bf16[64,1792]{1,0:T(8,128)(2,1)S(1)} %add_convert_fusion), channel_id=1, replica_groups=mesh['groups'=2,'seq'=4,'expert'=4] {'seq'}, dimensions={1}, use_global_device_ids=true | all-gather | bytes 1146880 | tf_op jit(solution)/shard_map/all_gather | solution.py:118
  186.3 0.3 fusion.16
  186.6 0.0 copy-start.1
  186.6 0.8 convolution_convert_fusion.1
  187.5 30.4 %all_to_all.10 = bf16[4,40,7168]{2,1,0:T(8,128)(2,1)S(1)} all-to-all(bf16[4,40,7168]{2,1,0:T(8,128)(2,1)S(1)} %bitcast.51), channel_id=1, replica_groups=mesh['groups'=2,'seq'=4,'expert'=4] {'expert'}, dimensions={0} | all-to-all | bytes 4587520 | tf_op jit(solution)/shard_map/all_to_all | solution.py:126
  217.8 0.8 fusion.12
  218.6 1.3 copy-done.11
  219.9 0.8 fusion.29
  220.7 1.3 copy-done.12
  221.9 2.2 convolution_convert_fusion
  224.1 0.0 reduce-scatter.5.cloned.1.call-update
  224.1 45.3 %reduce-scatter.5.cloned.1.call-done = bf16[4,40,1792]{2,1,0:T(8,128)(2,1)} async-done(((bf16[4,40,7168]{2,1,0:T(8,128)(2,1)}), bf16[4,40,1792]{2,1,0:T(8,128)(2,1)}) %reduce-scatter.5.cloned.1.call-update) | async-done | bytes 573456 | tf_op jit(solution)/shard_map/reduce_scatter | solution.py:20
  269.4 3.5 %all-to-all-start.1 = ((bf16[4,40,1792]{2,1,0:T(8,128)(2,1)}), bf16[4,40,1792]{2,1,0:T(8,128)(2,1)S(1)}, u32[]{:S(2)}, u32[]{:S(2)}) async-start(bf16[4,40,1792]{2,1,0:T(8,128)(2,1)} %reduce-scatter.5.cloned.1.call-done), calls=%async_computation.3 | async-start | bytes 1146880 | tf_op jit(solution)/shard_map/all_to_all | solution.py:23
  272.9 0.1 select_reduce_fusion
  273.1 9.2 %all-to-all-done.1 = bf16[4,40,1792]{2,1,0:T(8,128)(2,1)S(1)} async-done(((bf16[4,40,1792]{2,1,0:T(8,128)(2,1)}), bf16[4,40,1792]{2,1,0:T(8,128)(2,1)S(1)}, u32[]{:S(2)}, u32[]{:S(2)}) %all-to-all-start.1) | async-done | bytes 573472 | tf_op jit(solution)/shard_map/all_to_all | solution.py:23
  282.2 1.1 convolution_convert_fusion.3
  (29 shorter events, 0.2 us)
Async XLA Ops:
  7.2 20.2 %copy-start.2 = (bf16[64,16384]{1,0:T(8,128)(2,1)S(1)}, bf16[64,16384]{1,0:T(8,128)(2,1)}, u32[]{:S(2)}) copy-start(bf16[64,16384]{1,0:T(8,128)(2,1)} %param.17) | copy-start | bytes 6291460
  7.2 57.5 %all-gather.4.cloned.1.call-start = ((), (), s32[]{:S(2)}) async-start(), calls=%async_computation.4 | async-start | bytes 1638400 | tf_op jit(solution)/shard_map/all_gather | solution.py:69
  23.4 6.4 %copy-start.8 = (bf16[32,64]{1,0:T(8,128)(2,1)S(1)}, bf16[32,64]{1,0:T(8,128)(2,1)}, u32[]{:S(2)}) copy-start(bf16[32,64]{1,0:T(8,128)(2,1)} %param.22) | copy-start | bytes 12292
  24.5 19.3 %copy-start.6 = (bf16[256,64]{0,1:T(8,128)(2,1)S(1)}, bf16[256,64]{0,1:T(8,128)(2,1)}, u32[]{:S(2)}) copy-start(bf16[256,64]{0,1:T(8,128)(2,1)} %param.20) | copy-start | bytes 98308
  24.5 19.6 %copy-start.7 = (bf16[64,64]{1,0:T(8,128)(2,1)S(1)}, bf16[64,64]{1,0:T(8,128)(2,1)}, u32[]{:S(2)}) copy-start(bf16[64,64]{1,0:T(8,128)(2,1)} %param.25) | copy-start | bytes 24580
  25.6 34.5 %copy-start.4 = (bf16[64,2048]{1,0:T(8,128)(2,1)S(1)}, bf16[64,2048]{1,0:T(8,128)(2,1)}, u32[]{:S(2)}) copy-start(bf16[64,2048]{1,0:T(8,128)(2,1)} %param.18) | copy-start | bytes 786436
  27.3 103.3 %all-gather.6.cloned.1.call-start = ((), (), s32[]{:S(2)}) async-start(), calls=%async_computation.5 | async-start | bytes 2621440 | tf_op jit(solution)/shard_map/all_gather | solution.py:94
  73.7 4.0 %copy-start.13 = (bf16[1280,512]{1,0:T(8,128)(2,1)S(1)}, bf16[1280,512]{1,0:T(8,128)(2,1)}, u32[]{:S(2)}) copy-start(bf16[1280,512]{1,0:T(8,128)(2,1)} %all-gather.4.cloned.1.call-done) | copy-start | bytes 3932164
  77.7 4.6 %copy-start = (bf16[32,512,128]{2,1,0:T(8,128)(2,1)S(1)}, bf16[32,512,128]{2,1,0:T(8,128)(2,1)}, u32[]{:S(2)}) copy-start(bf16[32,512,128]{2,1,0:T(8,128)(2,1)} %param.26) | copy-start | bytes 12582916
  85.7 55.9 %copy-start.9 = (s32[64,2]{0,1:T(2,128)S(1)}, s32[64,2]{0,1:T(2,128)}, u32[]{:S(2)}) copy-start(s32[64,2]{0,1:T(2,128)} %param.29) | copy-start | bytes 1540
  85.7 78.6 %copy-start.5 = (bf16[64,1792]{1,0:T(8,128)(2,1)S(1)}, bf16[64,1792]{1,0:T(8,128)(2,1)}, u32[]{:S(2)}) copy-start(bf16[64,1792]{1,0:T(8,128)(2,1)} %param.28) | copy-start | bytes 688132
  85.7 78.6 %reduce-scatter.3.cloned.1.call-start = ((), (), s32[]{:S(2)}) async-start(), calls=%async_computation.6 | async-start | bytes 1146880 | tf_op jit(solution)/shard_map/reduce_scatter | solution.py:96
  141.4 128.1 %reduce-scatter.5.cloned.1.call-start = ((), (), s32[]{:S(2)}) async-start(), calls=%async_computation.7 | async-start | bytes 2867200 | tf_op jit(solution)/shard_map/reduce_scatter | solution.py:20
  165.3 52.5 %copy-start.3 = (bf16[64,1792]{1,0:T(8,128)(2,1)}, bf16[64,1792]{1,0:T(8,128)(2,1)S(1)}, u32[]{:S(2)}) copy-start(bf16[64,1792]{1,0:T(8,128)(2,1)S(1)} %add_convert_fusion) | copy-start | bytes 688132
  186.6 31.2 %copy-start.1 = (bf16[1,7168,256]{2,1,0:T(8,128)(2,1)S(1)}, bf16[1,7168,256]{2,1,0:T(8,128)(2,1)}, u32[]{:S(2)}) copy-start(bf16[1,7168,256]{2,1,0:T(8,128)(2,1)} %param.31) | copy-start | bytes 11010052
  217.8 2.0 copy-start.11
  219.9 2.0 copy-start.12
  221.9 51.0 %copy-start.10 = (f32[64,2]{0,1:T(2,128)S(1)}, f32[64,2]{0,1:T(2,128)}, u32[]{:S(2)}) copy-start(f32[64,2]{0,1:T(2,128)} %param.30) | copy-start | bytes 1540
  269.4 12.8 %all-to-all-start.1 = ((bf16[4,40,1792]{2,1,0:T(8,128)(2,1)}), bf16[4,40,1792]{2,1,0:T(8,128)(2,1)S(1)}, u32[]{:S(2)}, u32[]{:S(2)}) async-start(bf16[4,40,1792]{2,1,0:T(8,128)(2,1)} %reduce-scatter.5.cloned.1.call-done), calls=%async_computation.3 | async-start | bytes 1146880 | tf_op jit(solution)/shard_map/all_to_all | solution.py:23
Sparse Core Ops, SparseCore 0:
  27.4 37.1 all-gather.3
  85.8 44.7 all-gather.5
  141.5 22.7 reduce-scatter.2
  224.3 45.1 reduce-scatter.4
where the time goes:
time: 290 us
  waiting for transfers between devices  125 us (43%)
  blocking collectives  95.5 us (33%)
  matrix products  32.4 us (11%)
  between operations  14.9 us (5%)
  local copies, waits for them, and re-layouts  9.37 us (3%)
  other arithmetic  8.86 us (3%)
  starting transfers between devices  3.86 us (1%)
    reduce_scatter x1, waiting for transfers between devices, run_expert(): lax.psum_scatter(partial_out.astype(jnp.bfloat16), 'seq', scatter_dimensi...  45.3 us
    all_gather x1, waiting for transfers between devices, on_device(): all_values = lax.all_gather(head_vals, 'seq', axis=0, tiled=True)  44.8 us
    all_to_all x1, blocking collectives, on_device(): lax.all_to_all(outgoing, 'expert', split_axis=0, concat_axis=0, tiled=True)  30.4 us
    reduce_scatter x1, waiting for transfers between devices, on_device(): lax.psum_scatter(jnp.dot(all_values, w_out, preferred_element_type=jnp.fl...  21.6 us
    all_gather x1, blocking collectives, on_device(): lax.all_gather(attn_residual, 'seq', axis=1, tiled=True).astype(jnp.float32)  21 us
    all_gather x1, blocking collectives, on_device(): piece_rope = lax.all_gather(local_rope, 'seq', axis=0, tiled=True)  15.6 us
    all_gather x1, blocking collectives, on_device(): lax.all_gather(tool_lat, 'seq', axis=0, tiled=True)  15.3 us
    all_gather x1, blocking collectives, on_device(): lax.all_gather(tool_rope, 'seq', axis=0, tiled=True)  13.2 us
  transfers between devices with their start and end apart: 5, of which 5 were waited for; matrix products, arithmetic and copies ran while one was open for 2% of the time, Pallas kernels for 0%

commit v1 on v0

--- a/solution.py
+++ b/solution.py
@@ -91,7 +91,21 @@
         "thc,hcv->thv", latent_out, w_uv, preferred_element_type=jnp.float32
     ).astype(jnp.bfloat16)
     head_vals = head_vals.reshape(query_dev, heads_dev * value_width)
-    all_values = lax.all_gather(head_vals, "seq", axis=0, tiled=True)
+    ways, here, lap = (lax.axis_size("seq"), lax.axis_index("seq"), head_vals.shape[0])
+    lengths = [n * ways if d == 0 else n for d, n in enumerate(head_vals.shape)]
+    full = lax.dynamic_update_slice_in_dim(
+        jnp.zeros(lengths, head_vals.dtype), head_vals, here * lap, axis=0
+    )
+    going_up = going_down = head_vals
+    for far in range(1, ways // 2 + 1):
+        going_up = lax.ppermute(going_up, "seq", [(d, (d + 1) % ways) for d in range(ways)])
+        full = lax.dynamic_update_slice_in_dim(full, going_up, (here - far) % ways * lap, axis=0)
+        if 2 * far < ways:
+            going_down = lax.ppermute(going_down, "seq", [(d, (d - 1) % ways) for d in range(ways)])
+            full = lax.dynamic_update_slice_in_dim(
+                full, going_down, (here + far) % ways * lap, axis=0
+            )
+    all_values = full
     tok_dev = resid.shape[0]
     attn_sum = lax.psum_scatter(
         jnp.dot(all_values, w_out, preferred_element_type=jnp.float32).astype(jnp.bfloat16),

time: 290 us -> 277 us (0.955)
  waiting for transfers between devices: 125 us -> 113 us
  starting transfers between devices: 3.86 us -> 7.48 us
  matrix products: 32.4 us -> 29.3 us
    all_gather x1 -> x0, waiting for transfers between devices: 44.8 us -> none  [on_device(): all_values = lax.all_gather(head_vals, 'seq', axis=0, tiled=True)]
    ppermute x0 -> x3, waiting for transfers between devices: none -> 32.8 us  [the longest x2 23 us: on_device(): lax.ppermute(going_up, 'seq', [(d, (d + 1) % ways) for d in range(ways)])]
    ppermute x0 -> x3, starting transfers between devices: none -> 3.88 us  [the longest x1 2.91 us: on_device(): lax.ppermute(going_down, 'seq', [(d, (d - 1) % ways) for d in range(ways)])]
  transfers between devices with their start and end apart: 5 -> 7, of which waited for: 5 -> 7; matrix products, arithmetic and copies ran while one was open for 2% -> 2% of each run, Pallas kernels for 0% -> 0%
where the time goes in v1:
time: 277 us
  waiting for transfers between devices  113 us (41%)
  blocking collectives  96 us (35%)
  matrix products  29.3 us (11%)
  between operations  15 us (5%)
  local copies, waits for them, and re-layouts  8.99 us (3%)
  starting transfers between devices  7.48 us (3%)
  other arithmetic  6.98 us (3%)
    reduce_scatter x1, waiting for transfers between devices, run_expert(): lax.psum_scatter(partial_out.astype(jnp.bfloat16), 'seq', scatter_dimensi...  45.3 us
    all_to_all x1, blocking collectives, on_device(): lax.all_to_all(outgoing, 'expert', split_axis=0, concat_axis=0, tiled=True)  30.5 us
    ppermute x2, waiting for transfers between devices, on_device(): lax.ppermute(going_up, 'seq', [(d, (d + 1) % ways) for d in range(ways)])  23 us
    reduce_scatter x1, waiting for transfers between devices, on_device(): lax.psum_scatter(jnp.dot(all_values, w_out, preferred_element_type=jnp.fl...  21.8 us
    all_gather x1, blocking collectives, on_device(): lax.all_gather(attn_residual, 'seq', axis=1, tiled=True).astype(jnp.float32)  21.2 us
    all_gather x1, blocking collectives, on_device(): piece_rope = lax.all_gather(local_rope, 'seq', axis=0, tiled=True)  15.5 us
    all_gather x1, blocking collectives, on_device(): lax.all_gather(tool_lat, 'seq', axis=0, tiled=True)  15.3 us
    all_gather x1, blocking collectives, on_device(): lax.all_gather(tool_rope, 'seq', axis=0, tiled=True)  13.4 us
  transfers between devices with their start and end apart: 7, of which 7 were waited for; matrix products, arithmetic and copies ran while one was open for 2% of the time, Pallas kernels for 0%

profile of v1, /device:TPU:0, one launch (start us, length us, event | category | flops | bytes accessed | tf_op | source)
XLA Modules:
  0.0 276.6 jit_solution(13854912408070986237)
XLA Ops:
  7.2 0.0 all-gather.3.cloned.1.call-start
  8.1 15.3 %all_gather.15 = bf16[128,512]{1,0:T(8,128)(2,1)S(1)} all-gather(bf16[32,512]{1,0:T(8,128)(2,1)} %param.21), channel_id=1, replica_groups=mesh['groups'=2,'seq'=4,'expert'=4] {'seq'}, dimensions={0}, use_global_device_ids=true | all-gather | bytes 163840 | tf_op jit(solution)/shard_map/all_gather | solution.py:51
  23.4 1.2 gather_fusion
  24.6 0.1 select_select_fusion
  24.7 0.0 copy-start.11
  24.7 0.7 pad_maximum_fusion
  25.5 0.0 all-gather.3.cloned.1.call-update
  25.5 0.0 copy-start.10
  25.5 0.0 reduce-scatter.3.cloned.1.call-start
  25.6 0.0 copy-start.5
  25.6 2.3 reshape.119
  28.0 13.4 %all_gather.17 = bf16[128,64]{1,0:T(8,128)(2,1)S(1)} all-gather(bf16[32,64]{1,0:T(8,128)(2,1)S(1)} %copy-done.11), channel_id=1, replica_groups=mesh['groups'=2,'seq'=4,'expert'=4] {'seq'}, dimensions={0}, use_global_device_ids=true | all-gather | bytes 20480 | tf_op jit(solution)/shard_map/all_gather | solution.py:52
  41.4 0.9 gather_fusion.1
  42.2 0.1 copy.58
  42.4 0.1 select_select_fusion.1
  42.6 0.1 copy.59
  42.7 15.5 %all-gather = bf16[4,320,64]{1,2,0:T(8,128)(2,1)S(1)} all-gather(bf16[1,320,64]{1,2,0:T(8,128)(2,1)S(1)} %copy.59), channel_id=1, replica_groups=mesh['groups'=2,'seq'=4,'expert'=4] {'seq'}, dimensions={0}, use_global_device_ids=true | all-gather | bytes 204800 | tf_op jit(solution)/shard_map/all_gather | solution.py:70
  58.2 0.2 copy.60
  58.4 0.2 reshape.143
  58.5 0.5 reshape.120
  59.1 3.7 %all-gather.3.cloned.1.call-done = bf16[1280,512]{1,0:T(8,128)(2,1)} async-done(((bf16[320,512]{1,0:T(8,128)(2,1)}), bf16[1280,512]{1,0:T(8,128)(2,1)}) %all-gather.3.cloned.1.call-update) | async-done | bytes 1310736 | tf_op jit(solution)/shard_map/all_gather | solution.py:69
  62.9 4.3 %fusion.51 = f32[1280,2048]{1,0:T(8,128)S(1)} fusion(bf16[1280,512]{1,0:T(8,128)(2,1)} %all-gather.3.cloned.1.call-done, bf16[2048,512]{1,0:T(8,128)(2,1)S(1)} %copy-done.3), kind=kOutput, calls=%fused_computation.84 | convolution fusion | flops 2684354560 | bytes 13893632 | tf_op jit(solution)/shard_map/qc,kc->qk/dot_general | solution.py:77
  67.1 4.1 %fusion.50 = (f32[2048]{0:T(1024)S(1)}, f32[2048,1280]{0,1:T(8,128)S(1)}) fusion(f32[1280,2048]{1,0:T(8,128)S(1)} %fusion.51, bf16[1280,64]{0,1:T(8,128)(2,1)S(1)} %reshape.143, bf16[2048,64]{1,0:T(8,128)(2,1)S(1)} %reshape.120, s32[2048]{0:T(1024)S(1)} %fusion.40, s32[1280]{0:T(1024)S(1)} %fusion.38, pred[1280]{0:T(1024)(128)(4,1)S(1)} %fusion.45), kind=kOutput, calls=%fused_computation.83 | convolution fusion | flops 351270912 | bytes 21420288 | tf_op jit(solution)/shard_map/qc,kc->qk/dot_general | solution.py:80
  71.2 3.9 %fusion = f32[2048]{0:T(1024)S(1)} fusion(f32[2048,1280]{0,1:T(8,128)S(1)} %get-tuple-element.3, f32[2048]{0:T(1024)S(1)} %broadcast_maximum_fusion, s32[2048]{0:T(1024)S(1)} %fusion.40, s32[1280]{0:T(1024)S(1)} %fusion.38, pred[1280]{0:T(1024)(128)(4,1)S(1)} %fusion.45), kind=kLoop, calls=%fused_computation.7 | loop fusion | flops 13105152 | bytes 10516736 | tf_op jit(solution)/shard_map/reduce_sum | solution.py:85
  75.2 0.0 copy-start
  75.2 4.5 %divide_convert_fusion = bf16[2048,512]{1,0:T(8,128)(2,1)S(1)} fusion(f32[2048]{0:T(1024)S(1)} %fusion, bf16[1280,512]{1,0:T(8,128)(2,1)S(1)} %copy-done.16, f32[2048,1280]{0,1:T(8,128)S(1)} %get-tuple-element.3, f32[2048]{0:T(1024)S(1)} %broadcast_maximum_fusion, s32[2048]{0:T(1024)S(1)} %fusion.40, s32[1280]{0:T(1024)S(1)} %fusion.38, ...), kind=kOutput, calls=%fused_computation.15 | convolution fusion | flops 2699558912 | bytes 13924608 | tf_op jit(solution)/shard_map/dot_general | solution.py:86
  79.7 2.5 fusion.23
  82.2 0.1 copy.75
  82.3 1.0 collective-permute-start
  83.3 2.9 %collective-permute-start.1 = (bf16[64,4096]{1,0:T(8,128)(2,1)S(1)}, bf16[64,4096]{1,0:T(8,128)(2,1)S(1)}, u32[]{:S(2)}, u32[]{:S(2)}) collective-permute-start(bf16[64,4096]{1,0:T(8,128)(2,1)S(1)} %bitcast.57), channel_id=1, source_target_pairs={{0,12},{4,0},{8,4},{12,8},{1,13},{5,1},{9,5},{13,9},{2,14},{6,2},{... | collective-permute-start | bytes 1572872 | tf_op jit(solution)/shard_map/ppermute | solution.py:104
  86.2 0.2 broadcast_in_dim.73
  86.4 0.1 constant_dynamic-update-slice_fusion.3
  86.6 12.4 %collective-permute-done = bf16[64,4096]{1,0:T(8,128)(2,1)S(1)} collective-permute-done((bf16[64,4096]{1,0:T(8,128)(2,1)S(1)}, bf16[64,4096]{1,0:T(8,128)(2,1)S(1)}, u32[]{:S(2)}, u32[]{:S(2)}) %collective-permute-start) | collective-permute-done | bytes 524320 | tf_op jit(solution)/shard_map/ppermute | solution.py:101
  99.0 9.8 %collective-permute-done.1 = bf16[64,4096]{1,0:T(8,128)(2,1)S(1)} collective-permute-done((bf16[64,4096]{1,0:T(8,128)(2,1)S(1)}, bf16[64,4096]{1,0:T(8,128)(2,1)S(1)}, u32[]{:S(2)}, u32[]{:S(2)}) %collective-permute-start.1) | collective-permute-done | bytes 524320 | tf_op jit(solution)/shard_map/ppermute | solution.py:104
  108.9 10.6 %collective-permute-done.2 = bf16[64,4096]{1,0:T(8,128)(2,1)S(1)} collective-permute-done((bf16[64,4096]{1,0:T(8,128)(2,1)S(1)}, bf16[64,4096]{1,0:T(8,128)(2,1)S(1)}, u32[]{:S(2)}, u32[]{:S(2)}) %collective-permute-start.2) | collective-permute-done | bytes 524320 | tf_op jit(solution)/shard_map/ppermute | solution.py:101
  119.5 8.3 %convolution_convert_fusion.2 = bf16[256,1792]{1,0:T(8,128)(2,1)} fusion(bf16[256,4096]{1,0:T(8,128)(2,1)S(1)} %constant_dynamic-update-slice_fusion, bf16[4096,1792]{1,0:T(8,128)(2,1)} %param.27), kind=kOutput, calls=%fused_computation.21 | convolution fusion | flops 3758555136 | bytes 17694720 | tf_op jit(solution)/shard_map/dot_general | solution.py:111
  127.9 0.0 reduce-scatter.3.cloned.1.call-update
  127.9 0.0 reduce-scatter.5.cloned.1.call-start
  128.0 0.1 copy.63
  128.1 0.1 eq.35
  128.2 0.1 fusion.35
  128.3 0.2 reduce_window_sum.11
  128.5 0.2 select_reduce_fusion.1
  128.6 0.1 reduce_sum.49
  128.8 0.1 copy.64
  128.9 0.1 fusion.34
  129.0 21.8 %reduce-scatter.3.cloned.1.call-done = bf16[64,1792]{1,0:T(8,128)(2,1)} async-done(((bf16[256,1792]{1,0:T(8,128)(2,1)}), bf16[64,1792]{1,0:T(8,128)(2,1)}) %reduce-scatter.3.cloned.1.call-update) | async-done | bytes 229392 | tf_op jit(solution)/shard_map/reduce_scatter | solution.py:110
  150.8 1.0 add_convert_fusion
  151.8 0.0 copy-start.4
  151.8 21.2 %all_gather.19 = bf16[64,7168]{1,0:T(8,128)(2,1)S(1)} all-gather(bf16[64,1792]{1,0:T(8,128)(2,1)S(1)} %add_convert_fusion), channel_id=1, replica_groups=mesh['groups'=2,'seq'=4,'expert'=4] {'seq'}, dimensions={1}, use_global_device_ids=true | all-gather | bytes 1146880 | tf_op jit(solution)/shard_map/all_gather | solution.py:132
  173.0 0.3 fusion.16
  173.3 0.8 convolution_convert_fusion.1
  174.2 30.5 %all_to_all.10 = bf16[4,40,7168]{2,1,0:T(8,128)(2,1)S(1)} all-to-all(bf16[4,40,7168]{2,1,0:T(8,128)(2,1)S(1)} %bitcast.53), channel_id=1, replica_groups=mesh['groups'=2,'seq'=4,'expert'=4] {'expert'}, dimensions={0} | all-to-all | bytes 4587520 | tf_op jit(solution)/shard_map/all_to_all | solution.py:140
  204.7 0.8 fusion.12
  205.4 1.3 copy-done.14
  206.7 0.8 fusion.29
  207.5 1.3 copy-done.15
  208.7 2.2 convolution_convert_fusion
  210.9 0.0 reduce-scatter.5.cloned.1.call-update
  210.9 45.3 %reduce-scatter.5.cloned.1.call-done = bf16[4,40,1792]{2,1,0:T(8,128)(2,1)} async-done(((bf16[4,40,7168]{2,1,0:T(8,128)(2,1)}), bf16[4,40,1792]{2,1,0:T(8,128)(2,1)}) %reduce-scatter.5.cloned.1.call-update) | async-done | bytes 573456 | tf_op jit(solution)/shard_map/reduce_scatter | solution.py:20
  256.2 3.5 %all-to-all-start.1 = ((bf16[4,40,1792]{2,1,0:T(8,128)(2,1)}), bf16[4,40,1792]{2,1,0:T(8,128)(2,1)S(1)}, u32[]{:S(2)}, u32[]{:S(2)}) async-start(bf16[4,40,1792]{2,1,0:T(8,128)(2,1)} %reduce-scatter.5.cloned.1.call-done), calls=%async_computation.3 | async-start | bytes 1146880 | tf_op jit(solution)/shard_map/all_to_all | solution.py:23
  259.8 0.1 select_reduce_fusion
  259.9 9.2 %all-to-all-done.1 = bf16[4,40,1792]{2,1,0:T(8,128)(2,1)S(1)} async-done(((bf16[4,40,1792]{2,1,0:T(8,128)(2,1)}), bf16[4,40,1792]{2,1,0:T(8,128)(2,1)S(1)}, u32[]{:S(2)}, u32[]{:S(2)}) %all-to-all-start.1) | async-done | bytes 573472 | tf_op jit(solution)/shard_map/all_to_all | solution.py:23
  269.0 1.1 convolution_convert_fusion.3
  (43 shorter events, 0.3 us)
Async XLA Ops:
  7.2 17.4 %copy-start.6 = (bf16[256,512]{1,0:T(8,128)(2,1)S(1)}, bf16[256,512]{1,0:T(8,128)(2,1)}, u32[]{:S(2)}) copy-start(bf16[256,512]{1,0:T(8,128)(2,1)} %param.19) | copy-start | bytes 786436
  7.2 17.5 %copy-start.8 = (bf16[64,512]{1,0:T(8,128)(2,1)S(1)}, bf16[64,512]{1,0:T(8,128)(2,1)}, u32[]{:S(2)}) copy-start(bf16[64,512]{1,0:T(8,128)(2,1)} %param.24) | copy-start | bytes 196612
  7.2 18.4 %copy-start.2 = (bf16[64,16384]{1,0:T(8,128)(2,1)S(1)}, bf16[64,16384]{1,0:T(8,128)(2,1)}, u32[]{:S(2)}) copy-start(bf16[64,16384]{1,0:T(8,128)(2,1)} %param.17) | copy-start | bytes 6291460
  7.2 55.7 %all-gather.3.cloned.1.call-start = ((), (), s32[]{:S(2)}) async-start(), calls=%async_computation.4 | async-start | bytes 1638400 | tf_op jit(solution)/shard_map/all_gather | solution.py:69
  24.7 3.3 %copy-start.11 = (bf16[32,64]{1,0:T(8,128)(2,1)S(1)}, bf16[32,64]{1,0:T(8,128)(2,1)}, u32[]{:S(2)}) copy-start(bf16[32,64]{1,0:T(8,128)(2,1)} %param.22) | copy-start | bytes 12292
  25.5 16.8 %copy-start.9 = (bf16[256,64]{0,1:T(8,128)(2,1)S(1)}, bf16[256,64]{0,1:T(8,128)(2,1)}, u32[]{:S(2)}) copy-start(bf16[256,64]{0,1:T(8,128)(2,1)} %param.20) | copy-start | bytes 98308
  25.5 17.0 %copy-start.10 = (bf16[64,64]{1,0:T(8,128)(2,1)S(1)}, bf16[64,64]{1,0:T(8,128)(2,1)}, u32[]{:S(2)}) copy-start(bf16[64,64]{1,0:T(8,128)(2,1)} %param.25) | copy-start | bytes 24580
  25.5 125.2 %reduce-scatter.3.cloned.1.call-start = ((), (), s32[]{:S(2)}) async-start(), calls=%async_computation.5 | async-start | bytes 1146880 | tf_op jit(solution)/shard_map/reduce_scatter | solution.py:110
  25.6 32.9 %copy-start.5 = (bf16[64,2048]{1,0:T(8,128)(2,1)S(1)}, bf16[64,2048]{1,0:T(8,128)(2,1)}, u32[]{:S(2)}) copy-start(bf16[64,2048]{1,0:T(8,128)(2,1)} %param.18) | copy-start | bytes 786436
  28.0 34.9 %copy-start.3 = (bf16[2048,512]{1,0:T(8,128)(2,1)S(1)}, bf16[2048,512]{1,0:T(8,128)(2,1)}, u32[]{:S(2)}) copy-start(bf16[2048,512]{1,0:T(8,128)(2,1)} %reshape.119) | copy-start | bytes 6291460
  71.2 3.9 %copy-start.16 = (bf16[1280,512]{1,0:T(8,128)(2,1)S(1)}, bf16[1280,512]{1,0:T(8,128)(2,1)}, u32[]{:S(2)}) copy-start(bf16[1280,512]{1,0:T(8,128)(2,1)} %all-gather.3.cloned.1.call-done) | copy-start | bytes 3932164
  75.2 4.5 %copy-start = (bf16[32,512,128]{2,1,0:T(8,128)(2,1)S(1)}, bf16[32,512,128]{2,1,0:T(8,128)(2,1)}, u32[]{:S(2)}) copy-start(bf16[32,512,128]{2,1,0:T(8,128)(2,1)} %param.26) | copy-start | bytes 12582916
  82.3 16.7 %collective-permute-start = (bf16[64,4096]{1,0:T(8,128)(2,1)S(1)}, bf16[64,4096]{1,0:T(8,128)(2,1)S(1)}, u32[]{:S(2)}, u32[]{:S(2)}) collective-permute-start(bf16[64,4096]{1,0:T(8,128)(2,1)S(1)} %bitcast.56), channel_id=1, source_target_pairs={{0,4},{4,8},{8,12},{12,0},{1,5},{5,9},{9,13},{13,1},{2,6},{6,10},{... | collective-permute-start | bytes 1572872 | tf_op jit(solution)/shard_map/ppermute | solution.py:101
  83.3 25.6 %collective-permute-start.1 = (bf16[64,4096]{1,0:T(8,128)(2,1)S(1)}, bf16[64,4096]{1,0:T(8,128)(2,1)S(1)}, u32[]{:S(2)}, u32[]{:S(2)}) collective-permute-start(bf16[64,4096]{1,0:T(8,128)(2,1)S(1)} %bitcast.57), channel_id=1, source_target_pairs={{0,12},{4,0},{8,4},{12,8},{1,13},{5,1},{9,5},{13,9},{2,14},{6,2},{... | collective-permute-start | bytes 1572872 | tf_op jit(solution)/shard_map/ppermute | solution.py:104
  99.0 20.5 %collective-permute-start.2 = (bf16[64,4096]{1,0:T(8,128)(2,1)S(1)}, bf16[64,4096]{1,0:T(8,128)(2,1)S(1)}, u32[]{:S(2)}, u32[]{:S(2)}) collective-permute-start(bf16[64,4096]{1,0:T(8,128)(2,1)S(1)} %collective-permute-done), channel_id=1, source_target_pairs={{0,4},{4,8},{8,12},{12,0},{1,5},{5,9},{9,13},{13,1},{2,6},{6,10},{... | collective-permute-start | bytes 1572872 | tf_op jit(solution)/shard_map/ppermute | solution.py:101
  119.5 8.4 %copy-start.12 = (s32[64,2]{0,1:T(2,128)S(1)}, s32[64,2]{0,1:T(2,128)}, u32[]{:S(2)}) copy-start(s32[64,2]{0,1:T(2,128)} %param.29) | copy-start | bytes 1540
  119.5 31.2 %copy-start.7 = (bf16[64,1792]{1,0:T(8,128)(2,1)S(1)}, bf16[64,1792]{1,0:T(8,128)(2,1)}, u32[]{:S(2)}) copy-start(bf16[64,1792]{1,0:T(8,128)(2,1)} %param.28) | copy-start | bytes 688132
  127.9 128.3 %reduce-scatter.5.cloned.1.call-start = ((), (), s32[]{:S(2)}) async-start(), calls=%async_computation.6 | async-start | bytes 2867200 | tf_op jit(solution)/shard_map/reduce_scatter | solution.py:20
  151.8 22.4 %copy-start.4 = (bf16[64,1792]{1,0:T(8,128)(2,1)}, bf16[64,1792]{1,0:T(8,128)(2,1)S(1)}, u32[]{:S(2)}) copy-start(bf16[64,1792]{1,0:T(8,128)(2,1)S(1)} %add_convert_fusion) | copy-start | bytes 688132
  174.1 30.5 %copy-start.1 = (bf16[1,7168,256]{2,1,0:T(8,128)(2,1)S(1)}, bf16[1,7168,256]{2,1,0:T(8,128)(2,1)}, u32[]{:S(2)}) copy-start(bf16[1,7168,256]{2,1,0:T(8,128)(2,1)} %param.31) | copy-start | bytes 11010052
  204.7 2.0 copy-start.14
  206.7 2.0 copy-start.15
  210.9 48.8 %copy-start.13 = (f32[64,2]{0,1:T(2,128)S(1)}, f32[64,2]{0,1:T(2,128)}, u32[]{:S(2)}) copy-start(f32[64,2]{0,1:T(2,128)} %param.30) | copy-start | bytes 1540
  256.2 12.8 %all-to-all-start.1 = ((bf16[4,40,1792]{2,1,0:T(8,128)(2,1)}), bf16[4,40,1792]{2,1,0:T(8,128)(2,1)S(1)}, u32[]{:S(2)}, u32[]{:S(2)}) async-start(bf16[4,40,1792]{2,1,0:T(8,128)(2,1)} %reduce-scatter.5.cloned.1.call-done), calls=%async_computation.3 | async-start | bytes 1146880 | tf_op jit(solution)/shard_map/all_to_all | solution.py:23
Sparse Core Ops, SparseCore 0:
  25.6 37.1 all-gather.2
  128.0 22.6 reduce-scatter.2
  211.1 45.1 reduce-scatter.4
